TPU v7x, 1024 devices: a whole 4x8x16 slice. The times are simulated.
1024 devices in a mesh: gx: 4 (over x), gy: 16 (over z_hi, y), gz: 16 (over z_lo, core).
Axes of the slice: x: 4, y: 8, z: 16 (z_hi: 2, z_lo: 8; z = z_hi * 8 + z_lo), core: 2. Of those that a mesh axis runs over, the one named last changes fastest.
Arguments:
- populations: float32 [19, 8, 256, 2048], P(None, 'gx', 'gy', 'gz'), may hold values from 0.1 to 12, as said below
- shear_rate: float32 [8, 256, 2048], P('gx', 'gy', 'gz'), may hold values from 1 to 1.9
- part_cell: int32 [8388608], P(('gx', 'gy', 'gz')), may hold values from 0 to 4095
- part_move: int32 [8388608], P(('gx', 'gy', 'gz')), may hold values from 0 to 6
- part_mask: int32 [8388608], P(('gx', 'gy', 'gz')), may hold values 0 or 1
- part_velocity: float32 [3, 8388608], P(None, ('gx', 'gy', 'gz')), may hold values from -6 to 6
- part_mass: float32 [8388608], P(('gx', 'gy', 'gz')), may hold values from 0.5 to 2
Outputs:
- populations_out: float32 [19, 8, 256, 2048], P(None, 'gx', 'gy', 'gz')
- sources: float32 [4, 8, 256, 2048], P(None, 'gx', 'gy', 'gz')
- velocity_out: float32 [3, 8388608], P(None, ('gx', 'gy', 'gz'))
Inputs may be any that keep to these rules, and one draw needn't show every extreme that they name: `populations`: each entry is a positive population; a node's 19 values sum to its density. `part_cell`: local index of the particle's cell in the brick of the device holding it, (x * 16 + y) * 128 + z. `part_move`: 0 stays; 1 and 2 move to the next node along +x and -x, 3 and 4 along +y and -y, 5 and 6 along +z and -z. `part_mask`: 1 marks a particle of the advanced subset.
All inputs are finite; a program needn't handle non-finite values. No bound on the sum of `part_mask` on one device may be relied on, other than what follows from the above.
Results may differ from a plain program's by a relative error of at most 0.0001.
Values sent between devices are 32-bit elements; how exact they have to be, the bound alone decides.
No kernel may reach another device: no remote copies, remote signals or barrier semaphores. Data moves between devices by JAX's collectives and lax.ppermute only.
A program may use at most 32 MiB of HBM per device.

v0:
```python
import jax
import jax.numpy as jnp
import numpy as np
from jax import lax
from jax.sharding import PartitionSpec as P

drag_factor = 0.5


def extended(block, sides, width):
    for axis, dim in sides:
        count = lax.axis_size(axis)
        forward = [(i, i + 1) for i in range(count - 1)]
        forward.append((count - 1, 0))
        backward = [(target, source) for source, target in forward]
        low = lax.ppermute(
            lax.slice_in_dim(block, block.shape[dim] - width, None, axis=dim), axis, forward
        )
        high = lax.ppermute(lax.slice_in_dim(block, 0, width, axis=dim), axis, backward)
        block = jnp.concatenate([low, block, high], axis=dim)
    return block


def lattice_tables():
    speeds = np.array(
        [
            [0, 0, 0],
            [1, 0, 0],
            [-1, 0, 0],
            [0, 1, 0],
            [0, -1, 0],
            [0, 0, 1],
            [0, 0, -1],
            [1, 1, 0],
            [-1, -1, 0],
            [1, -1, 0],
            [-1, 1, 0],
            [1, 0, 1],
            [-1, 0, -1],
            [1, 0, -1],
            [-1, 0, 1],
            [0, 1, 1],
            [0, -1, -1],
            [0, 1, -1],
            [0, -1, 1],
        ]
    )
    comp_x = speeds[:, 0]
    comp_y = speeds[:, 1]
    comp_z = speeds[:, 2]
    square = comp_x * comp_x + comp_y * comp_y + comp_z * comp_z
    polynomials = [
        np.ones(19),
        19.0 * square - 30.0,
        (21.0 * square * square - 53.0 * square + 24.0) / 2.0,
        comp_x,
        (5.0 * square - 9.0) * comp_x,
        comp_y,
        (5.0 * square - 9.0) * comp_y,
        comp_z,
        (5.0 * square - 9.0) * comp_z,
        3.0 * comp_x * comp_x - square,
        (3.0 * square - 5.0) * (3.0 * comp_x * comp_x - square),
        comp_y * comp_y - comp_z * comp_z,
        (3.0 * square - 5.0) * (comp_y * comp_y - comp_z * comp_z),
        comp_x * comp_y,
        comp_y * comp_z,
        comp_x * comp_z,
        comp_x * (comp_y * comp_y - comp_z * comp_z),
        comp_y * (comp_z * comp_z - comp_x * comp_x),
        comp_z * (comp_x * comp_x - comp_y * comp_y),
    ]
    basis = np.stack(polynomials)
    basis = basis / np.sqrt(np.sum(basis * basis, axis=1, keepdims=True))
    fixed_rates = np.array(
        [
            0.0,
            1.19,
            1.4,
            0.0,
            1.2,
            0.0,
            1.2,
            0.0,
            1.2,
            0.0,
            1.4,
            0.0,
            1.4,
            0.0,
            0.0,
            0.0,
            1.98,
            1.98,
            1.98,
        ]
    )
    shear_rows = np.zeros(19)
    shear_rows[[9, 11, 13, 14, 15]] = 1.0
    weights = np.array([1.0 / 3.0] + [1.0 / 18.0] * 6 + [1.0 / 36.0] * 12)
    return (speeds, basis, fixed_rates, shear_rows, weights)


def fluid_velocity(distribution):
    speeds = lattice_tables()[0]
    lattice_vel = jnp.asarray(speeds, jnp.float32)
    density = jnp.sum(distribution, axis=0)
    momentum = jnp.dot(lattice_vel.T, distribution, precision=lax.Precision.HIGHEST)
    return momentum / density


def collide_flat(distribution, shear_field):
    speeds, basis, fixed_rates, shear_rows, weights = lattice_tables()
    lattice_vel = jnp.asarray(speeds, jnp.float32)
    basis_mat = jnp.asarray(basis, jnp.float32)
    fixed_vec = jnp.asarray(fixed_rates, jnp.float32)
    shear_vec = jnp.asarray(shear_rows, jnp.float32)
    weight_vec = jnp.asarray(weights, jnp.float32)
    density = jnp.sum(distribution, axis=0)
    momentum = jnp.dot(lattice_vel.T, distribution, precision=lax.Precision.HIGHEST)
    velocity = momentum / density
    projected = jnp.dot(lattice_vel, velocity, precision=lax.Precision.HIGHEST)
    speed_sq = jnp.sum(velocity * velocity, axis=0)
    equilibrium = (
        weight_vec[:, None]
        * density
        * (1.0 + 3.0 * projected + 4.5 * projected * projected - 1.5 * speed_sq)
    )
    moments = jnp.dot(basis_mat, distribution - equilibrium, precision=lax.Precision.HIGHEST)
    relax_rates = fixed_vec[:, None] + shear_vec[:, None] * shear_field[None, :]
    return distribution - jnp.dot(
        basis_mat.T, relax_rates * moments, precision=lax.Precision.HIGHEST
    )


def collide_brick(distribution, shear_field):
    flat_result = collide_flat(
        distribution.reshape(distribution.shape[0], -1), shear_field.reshape(-1)
    )
    return flat_result.reshape(distribution.shape)


def stream_inward(padded, speeds):
    extents = padded.shape[1:]
    pieces = []
    for direction in range(19):
        shift_x = int(speeds[direction, 0])
        shift_y = int(speeds[direction, 1])
        shift_z = int(speeds[direction, 2])
        pieces.append(
            padded[
                direction,
                1 - shift_x : extents[0] - 1 - shift_x,
                1 - shift_y : extents[1] - 1 - shift_y,
                1 - shift_z : extents[2] - 1 - shift_z,
            ]
        )
    return jnp.stack(pieces)


def per_device(populations, shear_rate, part_cell, part_move, part_mask, part_velocity, part_mass):
    speeds = lattice_tables()[0]
    lattice_size = populations.shape[0]
    size_x, size_y, size_z = (populations.shape[1], populations.shape[2], populations.shape[3])
    collided = collide_brick(populations, shear_rate)
    current = populations
    for sweep_index in range(2):
        if sweep_index == 1:
            collided = collide_brick(current, shear_rate)
        padded = extended(collided, (("gx", 1), ("gy", 2), ("gz", 3)), 1)
        current = stream_inward(padded, speeds)
    velocity_flat = fluid_velocity(current.reshape(lattice_size, -1))
    sampled = jnp.take(velocity_flat, part_cell, axis=1)
    active = part_mask.astype(jnp.float32)
    new_velocity = part_velocity + drag_factor * active * (sampled - part_velocity)
    payload = jnp.concatenate(
        [part_mass * (part_velocity - new_velocity), (part_mass * active)[None]], 0
    )
    local_x = part_cell // (size_y * size_z)
    local_y = part_cell // size_z % size_y
    local_z = part_cell % size_z
    ghost_x = local_x + (part_move == 1).astype(jnp.int32) - (part_move == 2).astype(jnp.int32) + 1
    ghost_y = local_y + (part_move == 3).astype(jnp.int32) - (part_move == 4).astype(jnp.int32) + 1
    ghost_z = local_z + (part_move == 5).astype(jnp.int32) - (part_move == 6).astype(jnp.int32) + 1
    target = (ghost_x * (size_y + 2) + ghost_y) * (size_z + 2) + ghost_z
    ghosted = (
        jnp.zeros((4, (size_x + 2) * (size_y + 2) * (size_z + 2)), jnp.float32)
        .at[:, target]
        .add(payload)
    )
    ghosted = ghosted.reshape(4, size_x + 2, size_y + 2, size_z + 2)
    arrived = extended(ghosted, (("gx", 1), ("gy", 2), ("gz", 3)), 1)
    sources = ghosted[:, 1:-1, 1:-1, 1:-1]
    sources = sources.at[:, 0].add(arrived[:, 0, 2:-2, 2:-2])
    sources = sources.at[:, -1].add(arrived[:, -1, 2:-2, 2:-2])
    sources = sources.at[:, :, 0].add(arrived[:, 2:-2, 0, 2:-2])
    sources = sources.at[:, :, -1].add(arrived[:, 2:-2, -1, 2:-2])
    sources = sources.at[:, :, :, 0].add(arrived[:, 2:-2, 2:-2, 0])
    sources = sources.at[:, :, :, -1].add(arrived[:, 2:-2, 2:-2, -1])
    return (current, sources, new_velocity)


def solution(mesh):
    placed = (
        P(None, "gx", "gy", "gz"),
        P("gx", "gy", "gz"),
        P(("gx", "gy", "gz")),
        P(("gx", "gy", "gz")),
        P(("gx", "gy", "gz")),
        P(None, ("gx", "gy", "gz")),
        P(("gx", "gy", "gz")),
    )
    return jax.shard_map(
        per_device,
        mesh=mesh,
        in_specs=placed,
        out_specs=(
            P(None, "gx", "gy", "gz"),
            P(None, "gx", "gy", "gz"),
            P(None, ("gx", "gy", "gz")),
        ),
        check_vma=False,
    )
```

profile of v0, /device:TPU:6, one launch (start us, length us, event | category | flops | bytes accessed | tf_op | source)
XLA Modules:
  0.0 268.6 jit_solution(1689257330298716012)
XLA Ops:
  7.3 2.7 %collective-permute-start.1 = (f32[19,1,16,128]{3,2,1,0:T(8,128)S(1)}, f32[19,1,16,128]{3,2,1,0:T(8,128)S(1)}, u32[]{:S(2)}, u32[]{:S(2)}) collective-permute-start(f32[19,1,16,128]{3,2,1,0:T(8,128)S(1)} %get-tuple-element.163), channel_id=1, source_target_pairs={{256,0},{512,256},{768,512},{0,768},{257,1},{513,257},{769,513},{1... | collective-permute-start | bytes 466952 | tf_op jit(solution)/shard_map/ppermute | solution.py:19
  10.0 14.2 %collective-permute-start = (f32[19,1,16,128]{3,2,1,0:T(8,128)S(1)}, f32[19,1,16,128]{3,2,1,0:T(8,128)S(1)}, u32[]{:S(2)}, u32[]{:S(2)}) collective-permute-start(f32[19,1,16,128]{3,2,1,0:T(8,128)S(1)} %get-tuple-element.164), channel_id=1, source_target_pairs={{0,256},{256,512},{512,768},{768,0},{1,257},{257,513},{513,769},{7... | collective-permute-start | bytes 466952 | tf_op jit(solution)/shard_map/ppermute | solution.py:16
  24.4 2.6 collective-permute-done
  27.1 12.7 %collective-permute-start.3 = (f32[19,4,1,128]{3,2,1,0:T(1,128)S(1)}, f32[19,4,1,128]{3,2,1,0:T(1,128)S(1)}, u32[]{:S(2)}, u32[]{:S(2)}) collective-permute-start(f32[19,4,1,128]{3,2,1,0:T(1,128)S(1)} %get-tuple-element.151), channel_id=1, source_target_pairs={{16,0},{32,16},{48,32},{64,48},{80,64},{96,80},{112,96},{128,112},... | collective-permute-start | bytes 116744 | tf_op jit(solution)/shard_map/ppermute | solution.py:19
  39.8 1.9 collective-permute-start.2
  41.8 14.7 %collective-permute-done.2 = f32[19,4,1,128]{3,2,1,0:T(1,128)S(1)} collective-permute-done((f32[19,4,1,128]{3,2,1,0:T(1,128)S(1)}, f32[19,4,1,128]{3,2,1,0:T(1,128)S(1)}, u32[]{:S(2)}, u32[]{:S(2)}) %collective-permute-start.2) | collective-permute-done | bytes 38944 | tf_op jit(solution)/shard_map/ppermute | solution.py:16
  57.6 5.7 %collective-permute-start.5 = (f32[19,4,18,1]{0,1,3,2:T(4,128)S(1)}, f32[19,4,18,1]{0,1,3,2:T(4,128)S(1)}, u32[]{:S(2)}, u32[]{:S(2)}) collective-permute-start(f32[19,4,18,1]{0,1,3,2:T(4,128)S(1)} %copy.88), channel_id=1, source_target_pairs={{1,0},{2,1},{3,2},{4,3},{5,4},{6,5},{7,6},{8,7},{9,8},{10,9},{11,1... | collective-permute-start | bytes 16424 | tf_op jit(solution)/shard_map/ppermute | solution.py:19
  64.1 2.1 collective-permute-start.4
  67.4 8.7 %collective-permute-done.4 = f32[19,4,18,1]{0,1,3,2:T(4,128)S(1)} collective-permute-done((f32[19,4,18,1]{0,1,3,2:T(4,128)S(1)}, f32[19,4,18,1]{0,1,3,2:T(4,128)S(1)}, u32[]{:S(2)}, u32[]{:S(2)}) %collective-permute-start.4) | collective-permute-done | bytes 5504 | tf_op jit(solution)/shard_map/ppermute | solution.py:16
  80.1 5.5 %collective-permute-start.6 = (f32[19,1,16,128]{3,2,1,0:T(8,128)S(1)}, f32[19,1,16,128]{3,2,1,0:T(8,128)S(1)}, u32[]{:S(2)}, u32[]{:S(2)}) collective-permute-start(f32[19,1,16,128]{3,2,1,0:T(8,128)S(1)} %get-tuple-element.160), channel_id=1, source_target_pairs={{0,256},{256,512},{512,768},{768,0},{1,257},{257,513},{513,769},{7... | collective-permute-start | bytes 466952 | tf_op jit(solution)/shard_map/ppermute | solution.py:16
  85.7 1.9 collective-permute-start.7
  88.5 5.6 %collective-permute-done.7 = f32[19,1,16,128]{3,2,1,0:T(8,128)S(1)} collective-permute-done((f32[19,1,16,128]{3,2,1,0:T(8,128)S(1)}, f32[19,1,16,128]{3,2,1,0:T(8,128)S(1)}, u32[]{:S(2)}, u32[]{:S(2)}) %collective-permute-start.7) | collective-permute-done | bytes 155680 | tf_op jit(solution)/shard_map/ppermute | solution.py:19
  94.2 1.9 collective-permute-start.9
  96.1 3.9 %collective-permute-start.8 = (f32[19,4,1,128]{3,2,1,0:T(1,128)S(1)}, f32[19,4,1,128]{3,2,1,0:T(1,128)S(1)}, u32[]{:S(2)}, u32[]{:S(2)}) collective-permute-start(f32[19,4,1,128]{3,2,1,0:T(1,128)S(1)} %get-tuple-element.150), channel_id=1, source_target_pairs={{0,16},{16,32},{32,48},{48,64},{64,80},{80,96},{96,112},{112,128},... | collective-permute-start | bytes 116744 | tf_op jit(solution)/shard_map/ppermute | solution.py:16
  100.0 12.7 %collective-permute-done.8 = f32[19,4,1,128]{3,2,1,0:T(1,128)S(1)} collective-permute-done((f32[19,4,1,128]{3,2,1,0:T(1,128)S(1)}, f32[19,4,1,128]{3,2,1,0:T(1,128)S(1)}, u32[]{:S(2)}, u32[]{:S(2)}) %collective-permute-start.8) | collective-permute-done | bytes 38944 | tf_op jit(solution)/shard_map/ppermute | solution.py:16
  114.6 1.9 collective-permute-start.10
  116.5 10.4 %collective-permute-start.11 = (f32[19,4,18,1]{2,0,3,1:T(8,128)S(1)}, f32[19,4,18,1]{2,0,3,1:T(8,128)S(1)}, u32[]{:S(2)}, u32[]{:S(2)}) collective-permute-start(f32[19,4,18,1]{2,0,3,1:T(8,128)S(1)} %copy.92), channel_id=1, source_target_pairs={{1,0},{2,1},{3,2},{4,3},{5,4},{6,5},{7,6},{8,7},{9,8},{10,9},{11,1... | collective-permute-start | bytes 16424 | tf_op jit(solution)/shard_map/ppermute | solution.py:19
  127.0 1.5 collective-permute-done.11
  131.5 27.8 %gather_fusion = f32[8192,3]{1,0:T(8,128)} fusion(f32[3,4096]{0,1:T(8,128)S(1)} %copy.94, s32[8192]{0:T(1024)S(1)} %get-tuple-element.167), kind=kCustom, calls=%fused_computation | custom fusion | bytes 229376 | tf_op jit(solution)/shard_map/jit(_take)/gather | solution.py:173
  159.3 2.8 %copy.95 = f32[8192,3]{0,1:T(4,128)S(1)} copy(f32[8192,3]{1,0:T(8,128)} %gather_fusion) | data formatting | bytes 196608 | tf_op jit(solution)/shard_map/jit(_take)/gather | solution.py:173
  162.9 2.7 %copy.96 = f32[8192,4]{1,0:T(8,128)} copy(f32[8192,4]{0,1:T(4,128)S(1)} %maximum_bitcast_fusion) | data formatting | bytes 262144 | tf_op jit(solution)/shard_map/concatenate | solution.py:176
  165.6 46.8 %scatter_custom_fusion = f32[4,9360]{0,1:T(8,128)} fusion(s32[8192]{0:T(1024)S(1)} %get-tuple-element.168, f32[8192,4]{1,0:T(8,128)} %copy.96, f32[]{:T(128)} %constant.236.clone.1), kind=kCustom, calls=%fused_computation.7 | custom fusion | flops 32768 | bytes 150272 | tf_op jit(solution)/shard_map/scatter-add | solution.py:189
  212.4 3.1 %copy.97 = f32[4,9360]{1,0:T(4,128)S(1)} copy(f32[4,9360]{0,1:T(8,128)} %scatter_custom_fusion) | data formatting | bytes 299520 | tf_op jit(solution)/shard_map/scatter-add | solution.py:189
  215.9 1.9 collective-permute-start.12
  218.0 3.9 %collective-permute-start.13 = (f32[4,1,18,130]{3,2,1,0:T(8,128)S(1)}, f32[4,1,18,130]{3,2,1,0:T(8,128)S(1)}, u32[]{:S(2)}, u32[]{:S(2)}) collective-permute-start(f32[4,1,18,130]{3,2,1,0:T(8,128)S(1)} %get-tuple-element.157), channel_id=1, source_target_pairs={{256,0},{512,256},{768,512},{0,768},{257,1},{513,257},{769,513},{1... | collective-permute-start | bytes 112328 | tf_op jit(solution)/shard_map/ppermute | solution.py:19
  222.5 3.2 %collective-permute-done.13 = f32[4,1,18,130]{3,2,1,0:T(8,128)S(1)} collective-permute-done((f32[4,1,18,130]{3,2,1,0:T(8,128)S(1)}, f32[4,1,18,130]{3,2,1,0:T(8,128)S(1)}, u32[]{:S(2)}, u32[]{:S(2)}) %collective-permute-start.13) | collective-permute-done | bytes 37472 | tf_op jit(solution)/shard_map/ppermute | solution.py:19
  225.7 1.9 collective-permute-start.15
  227.7 3.9 %collective-permute-start.14 = (f32[4,6,1,130]{3,2,1,0:T(1,128)S(1)}, f32[4,6,1,130]{3,2,1,0:T(1,128)S(1)}, u32[]{:S(2)}, u32[]{:S(2)}) collective-permute-start(f32[4,6,1,130]{3,2,1,0:T(1,128)S(1)} %get-tuple-element.156), channel_id=1, source_target_pairs={{0,16},{16,32},{32,48},{48,64},{64,80},{80,96},{96,112},{112,128},... | collective-permute-start | bytes 37448 | tf_op jit(solution)/shard_map/ppermute | solution.py:16
  231.8 12.5 %collective-permute-done.14 = f32[4,6,1,130]{3,2,1,0:T(1,128)S(1)} collective-permute-done((f32[4,6,1,130]{3,2,1,0:T(1,128)S(1)}, f32[4,6,1,130]{3,2,1,0:T(1,128)S(1)}, u32[]{:S(2)}, u32[]{:S(2)}) %collective-permute-start.14) | collective-permute-done | bytes 12512 | tf_op jit(solution)/shard_map/ppermute | solution.py:16
  244.6 7.9 %collective-permute-start.17 = (f32[4,6,20,1]{3,2,1,0:T(8,128)S(1)}, f32[4,6,20,1]{3,2,1,0:T(8,128)S(1)}, u32[]{:S(2)}, u32[]{:S(2)}) collective-permute-start(f32[4,6,20,1]{3,2,1,0:T(8,128)S(1)} %get-tuple-element.153), channel_id=1, source_target_pairs={{1,0},{2,1},{3,2},{4,3},{5,4},{6,5},{7,6},{8,7},{9,8},{10,9},{11,1... | collective-permute-start | bytes 5768 | tf_op jit(solution)/shard_map/ppermute | solution.py:19
  252.4 1.9 collective-permute-start.16
  254.6 12.5 %collective-permute-done.16 = f32[4,6,20,1]{3,2,1,0:T(8,128)S(1)} collective-permute-done((f32[4,6,20,1]{3,2,1,0:T(8,128)S(1)}, f32[4,6,20,1]{3,2,1,0:T(8,128)S(1)}, u32[]{:S(2)}, u32[]{:S(2)}) %collective-permute-start.16) | collective-permute-done | bytes 1952 | tf_op jit(solution)/shard_map/ppermute | solution.py:16
  (164 shorter events, 23.2 us)
Async XLA Ops:
  0.6 23.6 %copy-start.1 = (s32[8192]{0:T(1024)S(1)}, s32[8192]{0:T(1024)}, u32[]{:S(2)}) copy-start(s32[8192]{0:T(1024)} %param.32) | copy-start | bytes 98308
  0.7 23.6 %copy-start.6 = (s32[8192]{0:T(1024)S(1)}, s32[8192]{0:T(1024)}, u32[]{:S(2)}) copy-start(s32[8192]{0:T(1024)} %param.33) | copy-start | bytes 98308
  1.7 40.1 %copy-start.2 = (f32[8192]{0:T(1024)S(1)}, f32[8192]{0:T(1024)}, u32[]{:S(2)}) copy-start(f32[8192]{0:T(1024)} %param.36) | copy-start | bytes 98308
  1.7 40.1 %copy-start.7 = (s32[8192]{0:T(1024)S(1)}, s32[8192]{0:T(1024)}, u32[]{:S(2)}) copy-start(s32[8192]{0:T(1024)} %param.34) | copy-start | bytes 98308
  7.3 19.7 %collective-permute-start.1 = (f32[19,1,16,128]{3,2,1,0:T(8,128)S(1)}, f32[19,1,16,128]{3,2,1,0:T(8,128)S(1)}, u32[]{:S(2)}, u32[]{:S(2)}) collective-permute-start(f32[19,1,16,128]{3,2,1,0:T(8,128)S(1)} %get-tuple-element.163), channel_id=1, source_target_pairs={{256,0},{512,256},{768,512},{0,768},{257,1},{513,257},{769,513},{1... | collective-permute-start | bytes 466952 | tf_op jit(solution)/shard_map/ppermute | solution.py:19
  10.0 16.9 %collective-permute-start = (f32[19,1,16,128]{3,2,1,0:T(8,128)S(1)}, f32[19,1,16,128]{3,2,1,0:T(8,128)S(1)}, u32[]{:S(2)}, u32[]{:S(2)}) collective-permute-start(f32[19,1,16,128]{3,2,1,0:T(8,128)S(1)} %get-tuple-element.164), channel_id=1, source_target_pairs={{0,256},{256,512},{512,768},{768,0},{1,257},{257,513},{513,769},{7... | collective-permute-start | bytes 466952 | tf_op jit(solution)/shard_map/ppermute | solution.py:16
  27.1 14.7 %collective-permute-start.3 = (f32[19,4,1,128]{3,2,1,0:T(1,128)S(1)}, f32[19,4,1,128]{3,2,1,0:T(1,128)S(1)}, u32[]{:S(2)}, u32[]{:S(2)}) collective-permute-start(f32[19,4,1,128]{3,2,1,0:T(1,128)S(1)} %get-tuple-element.151), channel_id=1, source_target_pairs={{16,0},{32,16},{48,32},{64,48},{80,64},{96,80},{112,96},{128,112},... | collective-permute-start | bytes 116744 | tf_op jit(solution)/shard_map/ppermute | solution.py:19
  39.8 16.7 %collective-permute-start.2 = (f32[19,4,1,128]{3,2,1,0:T(1,128)S(1)}, f32[19,4,1,128]{3,2,1,0:T(1,128)S(1)}, u32[]{:S(2)}, u32[]{:S(2)}) collective-permute-start(f32[19,4,1,128]{3,2,1,0:T(1,128)S(1)} %get-tuple-element.152), channel_id=1, source_target_pairs={{0,16},{16,32},{32,48},{48,64},{64,80},{80,96},{96,112},{112,128},... | collective-permute-start | bytes 116744 | tf_op jit(solution)/shard_map/ppermute | solution.py:16
  57.6 8.5 %collective-permute-start.5 = (f32[19,4,18,1]{0,1,3,2:T(4,128)S(1)}, f32[19,4,18,1]{0,1,3,2:T(4,128)S(1)}, u32[]{:S(2)}, u32[]{:S(2)}) collective-permute-start(f32[19,4,18,1]{0,1,3,2:T(4,128)S(1)} %copy.88), channel_id=1, source_target_pairs={{1,0},{2,1},{3,2},{4,3},{5,4},{6,5},{7,6},{8,7},{9,8},{10,9},{11,1... | collective-permute-start | bytes 16424 | tf_op jit(solution)/shard_map/ppermute | solution.py:19
  63.9 13.5 %copy-start.9 = (f32[3]{0:T(128)S(1)}, f32[3]{0:T(128)}, u32[]{:S(2)}) copy-start(f32[3]{0:T(128)} %constant.305) | copy-start | bytes 40
  63.9 13.5 %copy-start.10 = (f32[3]{0:T(128)S(1)}, f32[3]{0:T(128)}, u32[]{:S(2)}) copy-start(f32[3]{0:T(128)} %constant.303) | copy-start | bytes 40
  63.9 13.5 %copy-start.11 = (f32[3]{0:T(128)S(1)}, f32[3]{0:T(128)}, u32[]{:S(2)}) copy-start(f32[3]{0:T(128)} %constant.301) | copy-start | bytes 40
  63.9 13.5 %copy-start.12 = (f32[3]{0:T(128)S(1)}, f32[3]{0:T(128)}, u32[]{:S(2)}) copy-start(f32[3]{0:T(128)} %constant.299) | copy-start | bytes 40
  63.9 13.5 %copy-start.13 = (f32[3]{0:T(128)S(1)}, f32[3]{0:T(128)}, u32[]{:S(2)}) copy-start(f32[3]{0:T(128)} %constant.297) | copy-start | bytes 40
  64.0 13.5 %copy-start.14 = (f32[3]{0:T(128)S(1)}, f32[3]{0:T(128)}, u32[]{:S(2)}) copy-start(f32[3]{0:T(128)} %constant.295) | copy-start | bytes 40
  64.0 13.5 %copy-start.15 = (f32[3]{0:T(128)S(1)}, f32[3]{0:T(128)}, u32[]{:S(2)}) copy-start(f32[3]{0:T(128)} %constant.293) | copy-start | bytes 40
  64.0 13.5 %copy-start.16 = (f32[3]{0:T(128)S(1)}, f32[3]{0:T(128)}, u32[]{:S(2)}) copy-start(f32[3]{0:T(128)} %constant.291) | copy-start | bytes 40
  64.1 12.0 %collective-permute-start.4 = (f32[19,4,18,1]{0,1,3,2:T(4,128)S(1)}, f32[19,4,18,1]{0,1,3,2:T(4,128)S(1)}, u32[]{:S(2)}, u32[]{:S(2)}) collective-permute-start(f32[19,4,18,1]{0,1,3,2:T(4,128)S(1)} %copy.86), channel_id=1, source_target_pairs={{0,1},{1,2},{2,3},{3,4},{4,5},{5,6},{6,7},{7,8},{8,9},{9,10},{10,1... | collective-permute-start | bytes 16424 | tf_op jit(solution)/shard_map/ppermute | solution.py:16
  80.1 8.3 %collective-permute-start.6 = (f32[19,1,16,128]{3,2,1,0:T(8,128)S(1)}, f32[19,1,16,128]{3,2,1,0:T(8,128)S(1)}, u32[]{:S(2)}, u32[]{:S(2)}) collective-permute-start(f32[19,1,16,128]{3,2,1,0:T(8,128)S(1)} %get-tuple-element.160), channel_id=1, source_target_pairs={{0,256},{256,512},{512,768},{768,0},{1,257},{257,513},{513,769},{7... | collective-permute-start | bytes 466952 | tf_op jit(solution)/shard_map/ppermute | solution.py:16
  85.7 8.3 %collective-permute-start.7 = (f32[19,1,16,128]{3,2,1,0:T(8,128)S(1)}, f32[19,1,16,128]{3,2,1,0:T(8,128)S(1)}, u32[]{:S(2)}, u32[]{:S(2)}) collective-permute-start(f32[19,1,16,128]{3,2,1,0:T(8,128)S(1)} %get-tuple-element.159), channel_id=1, source_target_pairs={{256,0},{512,256},{768,512},{0,768},{257,1},{513,257},{769,513},{1... | collective-permute-start | bytes 466952 | tf_op jit(solution)/shard_map/ppermute | solution.py:19
  94.2 5.9 %collective-permute-start.9 = (f32[19,4,1,128]{3,2,1,0:T(1,128)S(1)}, f32[19,4,1,128]{3,2,1,0:T(1,128)S(1)}, u32[]{:S(2)}, u32[]{:S(2)}) collective-permute-start(f32[19,4,1,128]{3,2,1,0:T(1,128)S(1)} %get-tuple-element.149), channel_id=1, source_target_pairs={{16,0},{32,16},{48,32},{64,48},{80,64},{96,80},{112,96},{128,112},... | collective-permute-start | bytes 116744 | tf_op jit(solution)/shard_map/ppermute | solution.py:19
  96.1 16.7 %collective-permute-start.8 = (f32[19,4,1,128]{3,2,1,0:T(1,128)S(1)}, f32[19,4,1,128]{3,2,1,0:T(1,128)S(1)}, u32[]{:S(2)}, u32[]{:S(2)}) collective-permute-start(f32[19,4,1,128]{3,2,1,0:T(1,128)S(1)} %get-tuple-element.150), channel_id=1, source_target_pairs={{0,16},{16,32},{32,48},{48,64},{64,80},{80,96},{96,112},{112,128},... | collective-permute-start | bytes 116744 | tf_op jit(solution)/shard_map/ppermute | solution.py:16
  114.6 14.5 %collective-permute-start.10 = (f32[19,4,18,1]{2,0,3,1:T(8,128)S(1)}, f32[19,4,18,1]{2,0,3,1:T(8,128)S(1)}, u32[]{:S(2)}, u32[]{:S(2)}) collective-permute-start(f32[19,4,18,1]{2,0,3,1:T(8,128)S(1)} %copy.90), channel_id=1, source_target_pairs={{0,1},{1,2},{2,3},{3,4},{4,5},{5,6},{6,7},{7,8},{8,9},{9,10},{10,1... | collective-permute-start | bytes 16424 | tf_op jit(solution)/shard_map/ppermute | solution.py:16
  116.5 12.0 %collective-permute-start.11 = (f32[19,4,18,1]{2,0,3,1:T(8,128)S(1)}, f32[19,4,18,1]{2,0,3,1:T(8,128)S(1)}, u32[]{:S(2)}, u32[]{:S(2)}) collective-permute-start(f32[19,4,18,1]{2,0,3,1:T(8,128)S(1)} %copy.92), channel_id=1, source_target_pairs={{1,0},{2,1},{3,2},{4,3},{5,4},{6,5},{7,6},{8,7},{9,8},{10,9},{11,1... | collective-permute-start | bytes 16424 | tf_op jit(solution)/shard_map/ppermute | solution.py:19
  130.5 31.6 %copy-start.26 = (f32[19,2,16,128]{3,2,1,0:T(8,128)}, f32[19,2,16,128]{3,2,1,0:T(8,128)S(1)}, u32[]{:S(2)}) copy-start(f32[19,2,16,128]{3,2,1,0:T(8,128)S(1)} %get-tuple-element.89) | copy-start | bytes 933892
  130.5 31.6 %copy-start.3 = (f32[3,8192]{1,0:T(4,128)S(1)}, f32[3,8192]{1,0:T(4,128)}, u32[]{:S(2)}) copy-start(f32[3,8192]{1,0:T(4,128)} %param.35) | copy-start | bytes 294916
  215.9 6.5 %collective-permute-start.12 = (f32[4,1,18,130]{3,2,1,0:T(8,128)S(1)}, f32[4,1,18,130]{3,2,1,0:T(8,128)S(1)}, u32[]{:S(2)}, u32[]{:S(2)}) collective-permute-start(f32[4,1,18,130]{3,2,1,0:T(8,128)S(1)} %get-tuple-element.158), channel_id=1, source_target_pairs={{0,256},{256,512},{512,768},{768,0},{1,257},{257,513},{513,769},{7... | collective-permute-start | bytes 112328 | tf_op jit(solution)/shard_map/ppermute | solution.py:16
  218.0 7.7 %collective-permute-start.13 = (f32[4,1,18,130]{3,2,1,0:T(8,128)S(1)}, f32[4,1,18,130]{3,2,1,0:T(8,128)S(1)}, u32[]{:S(2)}, u32[]{:S(2)}) collective-permute-start(f32[4,1,18,130]{3,2,1,0:T(8,128)S(1)} %get-tuple-element.157), channel_id=1, source_target_pairs={{256,0},{512,256},{768,512},{0,768},{257,1},{513,257},{769,513},{1... | collective-permute-start | bytes 112328 | tf_op jit(solution)/shard_map/ppermute | solution.py:19
  225.7 6.0 %collective-permute-start.15 = (f32[4,6,1,130]{3,2,1,0:T(1,128)S(1)}, f32[4,6,1,130]{3,2,1,0:T(1,128)S(1)}, u32[]{:S(2)}, u32[]{:S(2)}) collective-permute-start(f32[4,6,1,130]{3,2,1,0:T(1,128)S(1)} %get-tuple-element.155), channel_id=1, source_target_pairs={{16,0},{32,16},{48,32},{64,48},{80,64},{96,80},{112,96},{128,112},... | collective-permute-start | bytes 37448 | tf_op jit(solution)/shard_map/ppermute | solution.py:19
  227.7 16.6 %collective-permute-start.14 = (f32[4,6,1,130]{3,2,1,0:T(1,128)S(1)}, f32[4,6,1,130]{3,2,1,0:T(1,128)S(1)}, u32[]{:S(2)}, u32[]{:S(2)}) collective-permute-start(f32[4,6,1,130]{3,2,1,0:T(1,128)S(1)} %get-tuple-element.156), channel_id=1, source_target_pairs={{0,16},{16,32},{32,48},{48,64},{64,80},{80,96},{96,112},{112,128},... | collective-permute-start | bytes 37448 | tf_op jit(solution)/shard_map/ppermute | solution.py:16
  244.6 22.7 %collective-permute-start.17 = (f32[4,6,20,1]{3,2,1,0:T(8,128)S(1)}, f32[4,6,20,1]{3,2,1,0:T(8,128)S(1)}, u32[]{:S(2)}, u32[]{:S(2)}) collective-permute-start(f32[4,6,20,1]{3,2,1,0:T(8,128)S(1)} %get-tuple-element.153), channel_id=1, source_target_pairs={{1,0},{2,1},{3,2},{4,3},{5,4},{6,5},{7,6},{8,7},{9,8},{10,9},{11,1... | collective-permute-start | bytes 5768 | tf_op jit(solution)/shard_map/ppermute | solution.py:19
  252.4 14.6 %collective-permute-start.16 = (f32[4,6,20,1]{3,2,1,0:T(8,128)S(1)}, f32[4,6,20,1]{3,2,1,0:T(8,128)S(1)}, u32[]{:S(2)}, u32[]{:S(2)}) collective-permute-start(f32[4,6,20,1]{3,2,1,0:T(8,128)S(1)} %get-tuple-element.154), channel_id=1, source_target_pairs={{0,1},{1,2},{2,3},{3,4},{4,5},{5,6},{6,7},{7,8},{8,9},{9,10},{10,1... | collective-permute-start | bytes 5768 | tf_op jit(solution)/shard_map/ppermute | solution.py:16
  (17 other events, 198.7 us)
where the time goes:
time: 269 us
  starting transfers between devices  86.4 us (32%)
  waiting for transfers between devices  75.5 us (28%)
  other arithmetic  51.4 us (19%)
  local copies, waits for them, and re-layouts  48 us (18%)
  matrix products  5.69 us (2%)
    ppermute x9, waiting for transfers between devices, extended(): lax.ppermute(lax.slice_in_dim(block, block.shape[dim] - width, None, axis...  65.1 us
    ppermute x9, starting transfers between devices, extended(): lax.ppermute(lax.slice_in_dim(block, 0, width, axis=dim), axis, backward)  49.1 us
    scatter-add x1, other arithmetic, per_device(): ghosted = jnp.zeros((4, (size_x + 2) * (size_y + 2) * (size_z + 2)), jnp....  46.8 us
    ppermute x9, starting transfers between devices, extended(): lax.ppermute(lax.slice_in_dim(block, block.shape[dim] - width, None, axis...  37.3 us
    gather x2, local copies, waits for them, and re-layouts, per_device(): sampled = jnp.take(velocity_flat, part_cell, axis=1)  30.6 us
    ppermute x9, waiting for transfers between devices, extended(): lax.ppermute(lax.slice_in_dim(block, 0, width, axis=dim), axis, backward)  10.3 us
  transfers between devices with their start and end apart: 18, of which 11 were waited for; matrix products, arithmetic and copies ran while one was open for 1% of the time, Pallas kernels for 0%

commit v1 on v0

v1 whole, which is shorter than its diff:
```python
import jax
import jax.numpy as jnp
from jax import lax
from jax.experimental import pallas as pl
from jax.experimental.pallas import tpu as pltpu
from jax.sharding import PartitionSpec as P

SPEEDS = (
    (0, 0, 0),
    (1, 0, 0),
    (-1, 0, 0),
    (0, 1, 0),
    (0, -1, 0),
    (0, 0, 1),
    (0, 0, -1),
    (1, 1, 0),
    (-1, -1, 0),
    (1, -1, 0),
    (-1, 1, 0),
    (1, 0, 1),
    (-1, 0, -1),
    (1, 0, -1),
    (-1, 0, 1),
    (0, 1, 1),
    (0, -1, -1),
    (0, 1, -1),
    (0, -1, 1),
)
SHEAR = 19
UP = [i for i in range(19) if SPEEDS[i][0] == 1]
FLAT = [i for i in range(19) if SPEEDS[i][0] == 0]
DOWN = [i for i in range(19) if SPEEDS[i][0] == -1]
X_LOW = [(f, -1) for f in UP + FLAT + [SHEAR]] + [(f, -2) for f in UP]
X_HIGH = [(f, 2) for f in DOWN + FLAT + [SHEAR]] + [(f, 3) for f in DOWN]
PAIRS = X_LOW + [(f, 0) for f in range(20)] + [(f, 1) for f in range(20)] + X_HIGH
INDEX = {pair: q for q, pair in enumerate(PAIRS)}
FIRST = 42
DEP_LANE = 3 * (len(PAIRS) - FIRST)
Y_ROWS = 264
VMEM = pl.BlockSpec(memory_space=pltpu.VMEM)
SMEM = pl.BlockSpec(memory_space=pltpu.SMEM)


def relax(f, shear):
    s1, s2, s3 = f[1] + f[2], f[3] + f[4], f[5] + f[6]
    d1, d2, d3 = f[1] - f[2], f[3] - f[4], f[5] - f[6]
    e1, e2, e3 = f[7] + f[8], f[9] + f[10], f[11] + f[12]
    e4, e5, e6 = f[13] + f[14], f[15] + f[16], f[17] + f[18]
    g1, g2, g3 = f[7] - f[8], f[9] - f[10], f[11] - f[12]
    g4, g5, g6 = f[13] - f[14], f[15] - f[16], f[17] - f[18]
    exy, exz, eyz = e1 + e2, e3 + e4, e5 + e6
    s23, m23 = s2 + s3, s2 - s3
    axes = s1 + s23
    exx = exy + exz
    edges = exx + eyz
    rho = f[0] + axes + edges
    gp, gm = g1 + g2, g1 - g2
    hp, hm = g3 + g4, g3 - g4
    kp, km = g5 + g6, g5 - g6
    gx, gy, gz = gp + hp, gm + kp, hm + km
    jx, jy, jz = d1 + gx, d2 + gy, d3 + gz
    inv = 1.0 / rho
    ux, uy, uz = jx * inv, jy * inv, jz * inv
    xx, yy, zz = jx * ux, jy * uy, jz * uz
    sq = xx + yy + zz
    n1 = 8.0 * edges - 11.0 * axes - 30.0 * f[0] + (11.0 * rho - 19.0 * sq)
    n2 = 12.0 * f[0] - 4.0 * axes + edges - (3.0 * rho - 5.5 * sq)
    a9 = 2.0 * s1 - s23
    b9 = exx - 2.0 * eyz
    q9 = 3.0 * xx - sq
    b11 = exy - exz
    q11 = yy - zz
    t1 = n1 * (1.19 / 2394.0)
    t2 = n2 * (1.4 / 252.0)
    t4 = (gx - 4.0 * d1 + (2.0 / 3.0) * jx) * (1.2 / 40.0)
    t6 = (gy - 4.0 * d2 + (2.0 / 3.0) * jy) * (1.2 / 40.0)
    t8 = (gz - 4.0 * d3 + (2.0 / 3.0) * jz) * (1.2 / 40.0)
    t9 = (a9 + b9 - q9) * (shear * (1.0 / 36.0))
    t10 = (b9 - 2.0 * a9 + 0.5 * q9) * (1.4 / 72.0)
    t11 = (m23 + b11 - q11) * (shear * (1.0 / 12.0))
    t12 = (b11 - 2.0 * m23 + 0.5 * q11) * (1.4 / 24.0)
    quarter = shear * 0.25
    t13 = (e1 - e2 - jx * uy) * quarter
    t14 = (e5 - e6 - jy * uz) * quarter
    t15 = (e3 - e4 - jx * uz) * quarter
    t16 = (gp - hp) * (1.98 / 8.0)
    t17 = (kp - gm) * (1.98 / 8.0)
    t18 = (hm - km) * (1.98 / 8.0)
    axis = -11.0 * t1 - 4.0 * t2
    edge = 8.0 * t1 + t2
    p9 = t9 - 2.0 * t10
    p11 = t11 - 2.0 * t12
    r9 = t9 + t10
    r11 = t11 + t12
    out = [None] * 19
    out[0] = f[0] + 30.0 * t1 - 12.0 * t2

    def put(i, even, odd):
        out[i] = f[i] - (even + odd)
        out[i + 1] = f[i + 1] - (even - odd)

    put(1, axis + 2.0 * p9, -4.0 * t4)
    put(3, axis - p9 + p11, -4.0 * t6)
    put(5, axis - p9 - p11, -4.0 * t8)
    vxy, vxz, vyz = edge + r9 + r11, edge + r9 - r11, edge - 2.0 * r9
    put(7, vxy + t13, t4 + t6 + (t16 - t17))
    put(9, vxy - t13, t4 - t6 + (t16 + t17))
    put(11, vxz + t15, t4 + t8 - (t16 - t18))
    put(13, vxz - t15, t4 - t8 - (t16 + t18))
    put(15, vyz + t14, t6 + t8 + (t17 - t18))
    put(17, vyz - t14, t6 - t8 + (t17 + t18))
    return out


def collide_kernel(par, pops, shear, post, near, far):
    even = par[0] == 0
    for plane in range(2):
        for half in range(2):
            rows = slice(8 * half, 8 * half + 8)
            rate = shear[plane, rows, :]
            out = relax([pops[i, plane, rows, :] for i in range(19)], rate)
            for i in range(19):
                post[i, plane, rows, :] = out[i]

    def own(field, plane):
        return shear[plane] if field == SHEAR else post[field, plane]

    for slot in range(20):
        up = own(X_LOW[slot][0], X_LOW[slot][1] + 2)
        down = own(X_HIGH[slot][0], X_HIGH[slot][1] - 2)
        near[slot] = jnp.where(even, up, down)
        far[slot] = jnp.where(even, down, up)


def reader(par, post, shear, near, far):
    even = par[0] == 0

    def main(q, rows=slice(0, 16)):
        if q < 20:
            return jnp.where(even, far[q, rows, :], near[q, rows, :])
        if q >= 60:
            return jnp.where(even, near[q - 60, rows, :], far[q - 60, rows, :])
        field, plane = PAIRS[q]
        return shear[plane, rows, :] if field == SHEAR else post[field, plane, rows, :]

    return main


def z_pack_kernel(par, post, shear, xnear, xfar, dep, near, far):
    main = reader(par, post, shear, xnear, xfar)
    even = par[2] == 0
    lane = lax.broadcasted_iota(jnp.int32, (16, 128), 1)
    for tile in range(2):
        high = jnp.zeros((16, 128), jnp.float32)
        low = jnp.zeros((16, 128), jnp.float32)
        for slot in range(FIRST if tile == 0 else len(PAIRS) - FIRST):
            value = main(tile * FIRST + slot)
            mine = (lane >= 3 * slot) & (lane < 3 * slot + 3)
            high = jnp.where(mine, pltpu.roll(value, (3 * slot + 3) % 128, 1), high)
            low = jnp.where(mine, pltpu.roll(value, 3 * slot, 1), low)
        if tile == 1:
            for field in range(4):
                for plane in range(2):
                    spot = DEP_LANE + 2 * field + plane
                    here = lane == spot
                    up = dep[field, 5, plane]
                    down = dep[field, 6, plane]
                    high = jnp.where(here, pltpu.roll(up, spot + 1, 1), high)
                    low = jnp.where(here, pltpu.roll(down, spot, 1), low)
        near[tile] = jnp.where(even, high, low)
        far[tile] = jnp.where(even, low, high)


def y_pack_kernel(par, post, shear, xnear, xfar, znear, zfar, dep, near, far):
    main = reader(par, post, shear, xnear, xfar)
    even = par[1] == 0
    even_z = par[2] == 0

    def put(row, count, high, low):
        near[row : row + count, :] = jnp.where(even, high, low)
        far[row : row + count, :] = jnp.where(even, low, high)

    top, bottom = slice(13, 16), slice(0, 3)
    for q in range(len(PAIRS)):
        put(3 * q, 3, main(q, top), main(q, bottom))
    for field in range(4):
        for plane in range(2):
            row = 240 + 2 * field + plane
            put(row, 1, dep[field, 3, plane, 15:16, :], dep[field, 4, plane, 0:1, :])
    for tile in range(2):
        put(
            248 + 3 * tile,
            3,
            jnp.where(even_z, zfar[tile, top, :], znear[tile, top, :]),
            jnp.where(even_z, zfar[tile, bottom, :], znear[tile, bottom, :]),
        )
        put(
            254 + 3 * tile,
            3,
            jnp.where(even_z, znear[tile, top, :], zfar[tile, top, :]),
            jnp.where(even_z, znear[tile, bottom, :], zfar[tile, bottom, :]),
        )
    near[260:264, :] = jnp.zeros((4, 128), jnp.float32)
    far[260:264, :] = jnp.zeros((4, 128), jnp.float32)


def shifted(value, shift_y, shift_z):
    if shift_y:
        value = pltpu.roll(value, shift_y % 24, 0)
    if shift_z:
        value = pltpu.roll(value, shift_z % 256, 1)
    return value


def step_kernel(
    par,
    post,
    shear,
    xnear,
    xfar,
    znear,
    zfar,
    ynear,
    yfar,
    dep,
    pops_out,
    fluid,
    partial,
    snear,
    sfar,
    columns,
    field_ext,
    second,
):
    main = reader(par, post, shear, xnear, xfar)
    even_x, even_y, even_z = par[0] == 0, par[1] == 0, par[2] == 0

    def y_low(row, count):
        return jnp.where(even_y, yfar[row : row + count, :], ynear[row : row + count, :])

    def y_high(row, count):
        return jnp.where(even_y, ynear[row : row + count, :], yfar[row : row + count, :])

    zero = jnp.zeros((8, 128), jnp.float32)
    for tile in range(2):
        for side in range(2):
            a, b = (zfar, znear) if side == 0 else (znear, zfar)
            columns[side, tile, 0:16, :] = jnp.where(even_z, a[tile], b[tile])
            columns[side, tile, 16:24, :] = zero
            row = 248 + 6 * side + 3 * tile
            columns[side, tile, 16:19, :] = y_high(row, 3)
            columns[side, tile, 21:24, :] = y_low(row, 3)
    lane = lax.broadcasted_iota(jnp.int32, (24, 128), 1)
    for q in range(len(PAIRS)):
        tile, slot = (0, q) if q < FIRST else (1, q - FIRST)
        field_ext[q, 0:16, 0:128] = main(q)
        field_ext[q, 16:24, 0:128] = zero
        field_ext[q, 16:19, 0:128] = y_high(3 * q, 3)
        field_ext[q, 21:24, 0:128] = y_low(3 * q, 3)
        low = pltpu.roll(columns[0, tile], (125 - 3 * slot) % 128, 1)
        high = pltpu.roll(columns[1, tile], (-3 * slot) % 128, 1)
        field_ext[q, :, 128:256] = jnp.where(lane < 64, high, low)

    for plane in range(4):
        for i in range(19):
            cx, cy, cz = SPEEDS[i]
            value = field_ext[INDEX[(i, plane - 1 - cx)]]
            second[i, plane] = shifted(value, cy, cz).reshape(3, 8, 256)

    for plane in range(4):
        rates = INDEX[(SHEAR, plane - 1)]

        def body(t, carry, plane=plane, rates=rates):
            row = pl.multiple_of(t * 8, 8)
            for z in range(2):
                lanes = slice(128 * z, 128 * z + 128)
                rate = field_ext[rates, pl.ds(row, 8), lanes]
                out = relax([second[i, plane, t, :, lanes] for i in range(19)], rate)
                for i in range(19):
                    second[i, plane, t, :, lanes] = out[i]
            return carry

        lax.fori_loop(0, 3, body, 0)

    lane16 = lax.broadcasted_iota(jnp.int32, (16, 128), 1)
    row8 = lax.broadcasted_iota(jnp.int32, (8, 128), 0)
    totals = [[None, None] for _ in range(4)]
    ups, downs = [None] * 4, [None] * 4
    for plane in range(2):
        rho = jx = jy = jz = None

        def add(total, value, sign):
            if sign == 0:
                return total
            if total is None:
                return value if sign > 0 else -value
            return total + value if sign > 0 else total - value

        for i in range(19):
            cx, cy, cz = SPEEDS[i]
            value = shifted(second[i, plane + 1 - cx].reshape(24, 256), cy, cz)
            pops_out[i, plane] = value[0:16, 0:128]
            rho = add(rho, value, 1)
            jx, jy, jz = add(jx, value, cx), add(jy, value, cy), add(jz, value, cz)
        u = [jx / rho, jy / rho, jz / rho]
        for c in range(3):
            fluid[c, plane] = u[c][0:16, 0:128]

        def moved(k, speed):
            s = dep[3, k, plane]
            return [dep[c, k, plane] - speed[c] * s for c in range(3)] + [2.0 * s]

        inner = [u[c][0:16, 0:128] for c in range(3)]
        total = moved(0, inner)
        tops = moved(1, inner)
        bottoms = moved(2, inner)

        def y_ext(k):
            ghosts = []
            for c in range(4):
                row = 240 + 2 * c + plane
                if k == 3:
                    ghost = jnp.where(row8 == 7, jnp.broadcast_to(y_low(row, 1), (8, 128)), 0.0)
                else:
                    ghost = jnp.where(row8 == 0, jnp.broadcast_to(y_high(row, 1), (8, 128)), 0.0)
                ghosts.append(jnp.concatenate([dep[c, k, plane], ghost], 0))
            return ghosts

        def z_ext(k):
            ghosts = []
            for c in range(4):
                spot = DEP_LANE + 2 * c + plane
                if k == 5:
                    ghost = pltpu.roll(columns[0, 1, 0:16, :], (127 - spot) % 128, 1)
                    ghost = jnp.where(lane16 == 127, ghost, 0.0)
                else:
                    ghost = pltpu.roll(columns[1, 1, 0:16, :], (-spot) % 128, 1)
                    ghost = jnp.where(lane16 == 0, ghost, 0.0)
                ghosts.append(jnp.concatenate([dep[c, k, plane], ghost], 1))
            return ghosts

        for k, shift in ((3, 1), (4, 23)):
            v = y_ext(k)
            rows = [v[c] - jnp.where(v[3] != 0.0, u[c][:, 0:128] * v[3], 0.0) for c in range(3)]
            rows.append(2.0 * v[3])
            for c in range(4):
                total[c] = total[c] + pltpu.roll(rows[c], shift, 0)[0:16, :]
        for k, shift in ((5, 1), (6, 255)):
            v = z_ext(k)
            rows = [v[c] - jnp.where(v[3] != 0.0, u[c][0:16, :] * v[3], 0.0) for c in range(3)]
            rows.append(2.0 * v[3])
            for c in range(4):
                total[c] = total[c] + pltpu.roll(rows[c], shift, 1)[:, 0:128]
        for c in range(4):
            totals[c][plane] = total[c]
        if plane == 0:
            downs, held = bottoms, tops
        else:
            ups = tops
            for c in range(4):
                totals[c][0] = totals[c][0] + bottoms[c]
                totals[c][1] = totals[c][1] + held[c]
    for c in range(4):
        partial[c, 0] = totals[c][0]
        partial[c, 1] = totals[c][1]
        snear[c] = jnp.where(even_x, ups[c], downs[c])
        sfar[c] = jnp.where(even_x, downs[c], ups[c])


def join_kernel(par, partial, near, far, out):
    even = par[0] == 0
    for c in range(4):
        out[c, 0] = partial[c, 0] + jnp.where(even, far[c], near[c])
        out[c, 1] = partial[c, 1] + jnp.where(even, near[c], far[c])


def deposit_kernel(cell, move, mask, mass, velocity, out, picked, keys):
    where = cell[...]
    code = (move[...] * 32 + jnp.right_shift(where, 7)).astype(jnp.float32).astype(jnp.bfloat16)
    spot = jnp.bitwise_and(where, 127).astype(jnp.float32).astype(jnp.bfloat16)
    weight = 0.5 * mask[...].astype(jnp.float32) * mass[...]
    rows = lax.broadcasted_iota(jnp.int32, (256, where.shape[1]), 0)
    rows = rows.astype(jnp.float32).astype(jnp.bfloat16)
    one, zero = jnp.bfloat16(1), jnp.bfloat16(0)
    keys[...] = jnp.where(rows == code, one, zero)
    here = rows[0:128] == spot
    for c in range(4):
        value = weight * velocity[c : c + 1, :] if c < 3 else weight
        coarse = value.astype(jnp.bfloat16)
        fine = (value - coarse.astype(jnp.float32)).astype(jnp.bfloat16)
        picked[256 * c : 256 * c + 128, :] = jnp.where(here, coarse, zero)
        picked[256 * c + 128 : 256 * c + 256, :] = jnp.where(here, fine, zero)
    total = lax.dot_general(
        keys[...], picked[...], (((1,), (1,)), ((), ())), preferred_element_type=jnp.float32
    )
    for c in range(4):
        out[c] = total[:, 256 * c : 256 * c + 128] + total[:, 256 * c + 128 : 256 * c + 256]


def drag_kernel(cell, mask, velocity, fluid, out):
    for group in range(8):
        rows = slice(8 * group, 8 * group + 8)
        where = cell[rows, :]
        lane = jnp.bitwise_and(where, 127)
        line = jnp.right_shift(where, 7)
        picked = [jnp.zeros((8, 128), jnp.float32) for _ in range(3)]
        for r in range(32):
            mine = line == r
            for c in range(3):
                table = jnp.broadcast_to(fluid[c, r : r + 1, :], (8, 128))
                value = jnp.take_along_axis(table, lane, axis=1)
                picked[c] = jnp.where(mine, value, picked[c])
        half = 0.5 * mask[rows, :].astype(jnp.float32)
        for c in range(3):
            old = velocity[c, rows, :]
            out[c, rows, :] = old + half * (picked[c] - old)


def swap(value, axis, shifted_by_one):
    count = lax.axis_size(axis)
    pairs = []
    for i in range(count):
        if shifted_by_one:
            pairs.append((i, (i + 1) % count if i % 2 else (i - 1) % count))
        else:
            pairs.append((i, i ^ 1))
    return lax.ppermute(value, axis, pairs)


def both_swaps(near, far, axis):
    return swap(near, axis, False), swap(far, axis, True)


def cost(flops, size):
    return pl.CostEstimate(flops=flops, bytes_accessed=size, transcendentals=0)


def struct(*shape):
    return jax.ShapeDtypeStruct(shape, jnp.float32)


def per_device(populations, shear_rate, part_cell, part_move, part_mask, part_velocity, part_mass):
    par = jnp.stack([lax.axis_index(a) % 2 for a in ("gx", "gy", "gz")]).astype(jnp.int32)
    count = part_cell.shape[0]
    limit = pltpu.CompilerParams(vmem_limit_bytes=40 << 20)

    post, near, far = pl.pallas_call(
        collide_kernel,
        out_shape=(struct(19, 2, 16, 128), struct(20, 16, 128), struct(20, 16, 128)),
        in_specs=[SMEM, VMEM, VMEM],
        out_specs=(VMEM,) * 3,
        compiler_params=limit,
        cost_estimate=cost(2000000, 2000000),
        name="collide",
    )(par, populations, shear_rate)
    xnear, xfar = both_swaps(near, far, "gx")

    flat = (1, count)
    dep = pl.pallas_call(
        deposit_kernel,
        out_shape=struct(4, 256, 128),
        in_specs=[VMEM] * 5,
        out_specs=VMEM,
        scratch_shapes=[
            pltpu.VMEM((1024, count), jnp.bfloat16),
            pltpu.VMEM((256, count), jnp.bfloat16),
        ],
        compiler_params=limit,
        cost_estimate=cost(4000000000, 1000000),
        name="deposit",
    )(
        part_cell.reshape(flat),
        part_move.reshape(flat),
        part_mask.reshape(flat),
        part_mass.reshape(flat),
        part_velocity,
    )
    dep = dep.reshape(4, 8, 2, 16, 128)

    near, far = pl.pallas_call(
        z_pack_kernel,
        out_shape=(struct(2, 16, 128), struct(2, 16, 128)),
        in_specs=[SMEM] + [VMEM] * 5,
        out_specs=(VMEM,) * 2,
        compiler_params=limit,
        cost_estimate=cost(500000, 1000000),
        name="z_pack",
    )(par, post, shear_rate, xnear, xfar, dep)
    znear, zfar = both_swaps(near, far, "gz")

    near, far = pl.pallas_call(
        y_pack_kernel,
        out_shape=(struct(Y_ROWS, 128), struct(Y_ROWS, 128)),
        in_specs=[SMEM] + [VMEM] * 7,
        out_specs=(VMEM,) * 2,
        compiler_params=limit,
        cost_estimate=cost(500000, 1000000),
        name="y_pack",
    )(par, post, shear_rate, xnear, xfar, znear, zfar, dep)
    ynear, yfar = both_swaps(near, far, "gy")

    populations_out, fluid, partial, near, far = pl.pallas_call(
        step_kernel,
        out_shape=(
            struct(19, 2, 16, 128),
            struct(3, 2, 16, 128),
            struct(4, 2, 16, 128),
            struct(4, 16, 128),
            struct(4, 16, 128),
        ),
        in_specs=[SMEM] + [VMEM] * 9,
        out_specs=(VMEM,) * 5,
        scratch_shapes=[
            pltpu.VMEM((2, 2, 24, 128), jnp.float32),
            pltpu.VMEM((len(PAIRS), 24, 256), jnp.float32),
            pltpu.VMEM((19, 4, 3, 8, 256), jnp.float32),
        ],
        compiler_params=limit,
        cost_estimate=cost(20000000, 4000000),
        name="step",
    )(par, post, shear_rate, xnear, xfar, znear, zfar, ynear, yfar, dep)
    snear, sfar = both_swaps(near, far, "gx")

    tall = (count // 128, 128)
    velocity_out = pl.pallas_call(
        drag_kernel,
        out_shape=struct(3, *tall),
        in_specs=[VMEM] * 4,
        out_specs=VMEM,
        compiler_params=limit,
        cost_estimate=cost(5000000, 1000000),
        name="drag",
    )(
        part_cell.reshape(tall),
        part_mask.reshape(tall),
        part_velocity.reshape(3, *tall),
        fluid.reshape(3, 32, 128),
    )
    velocity_out = velocity_out.reshape(3, count)

    sources = pl.pallas_call(
        join_kernel,
        out_shape=struct(4, 2, 16, 128),
        in_specs=[SMEM] + [VMEM] * 3,
        out_specs=VMEM,
        compiler_params=limit,
        cost_estimate=cost(100000, 300000),
        name="join",
    )(par, partial, snear, sfar)
    return populations_out, sources, velocity_out


def solution(mesh):
    placed = (
        P(None, "gx", "gy", "gz"),
        P("gx", "gy", "gz"),
        P(("gx", "gy", "gz")),
        P(("gx", "gy", "gz")),
        P(("gx", "gy", "gz")),
        P(None, ("gx", "gy", "gz")),
        P(("gx", "gy", "gz")),
    )
    return jax.shard_map(
        per_device,
        mesh=mesh,
        in_specs=placed,
        out_specs=(
            P(None, "gx", "gy", "gz"),
            P(None, "gx", "gy", "gz"),
            P(None, ("gx", "gy", "gz")),
        ),
        check_vma=False,
    )
```

time: 269 us -> 77.8 us (0.29)
  waiting for transfers between devices: 75.5 us -> 14.5 us
  other arithmetic: 51.4 us -> 0.08 us
  local copies, waits for them, and re-layouts: 48 us -> 2.34 us
  starting transfers between devices: 86.4 us -> 47.2 us
  Pallas kernels: 0 us -> 12.3 us
  matrix products: 5.69 us -> 0 us
    ppermute x18 -> x8, waiting for transfers between devices: 75.5 us -> 14.5 us  [swap(): return lax.ppermute(value, axis, pairs)]
    scatter-add x3 -> x0, other arithmetic: 46.9 us -> none  [the longest x1 46.8 us: per_device(): ghosted = jnp.zeros((4, (size_x + 2) * (size_y + 2) * (size_z + 2)), jnp....]
    ppermute x18 -> x8, starting transfers between devices: 86.4 us -> 47.2 us  [swap(): return lax.ppermute(value, axis, pairs)]
    gather x2 -> x0, local copies, waits for them, and re-layouts: 30.6 us -> none  [per_device(): sampled = jnp.take(velocity_flat, part_cell, axis=1)]
    pallas_call x0 -> x7, Pallas kernels: none -> 12.3 us  [the longest x1 4.53 us: per_device(): pl.pallas_call(deposit_kernel, out_shape=struct(4, 256, 128), in_specs=[V...]
    dot_general x7 -> x0, matrix products: 5.69 us -> none  [the longest x2 1.92 us: collide_flat(): jnp.dot(basis_mat, distribution - equilibrium, precision=lax.Precision.HI...]
    scatter-add x5 -> x0, local copies, waits for them, and re-layouts: 3.96 us -> none  [the longest x1 3.14 us: per_device(): ghosted = jnp.zeros((4, (size_x + 2) * (size_y + 2) * (size_z + 2)), jnp....]
    slice x16 -> x0, local copies, waits for them, and re-layouts: 3.63 us -> none  [the longest x11 2.26 us: extended(): lax.slice_in_dim(block, 0, width, axis=dim)]
  transfers between devices with their start and end apart: 18 -> 8, of which waited for: 11 -> 3; matrix products, arithmetic and copies ran while one was open for 1% -> 1% of each run, Pallas kernels for 0% -> 7%
where the time goes in v1:
time: 77.8 us; the launch traced here: 77.4 us
  starting transfers between devices  47.2 us (61%)
  waiting for transfers between devices  14.5 us (19%)
  Pallas kernels  12.3 us (16%)
  local copies, waits for them, and re-layouts  2.34 us (3%)
  between operations  0.86 us (1%)
    ppermute x8, starting transfers between devices, swap(): return lax.ppermute(value, axis, pairs)  47.2 us
    ppermute x8, waiting for transfers between devices, swap(): return lax.ppermute(value, axis, pairs)  14.5 us
    pallas_call x1, Pallas kernels, per_device(): pl.pallas_call(deposit_kernel, out_shape=struct(4, 256, 128), in_specs=[V...  4.53 us
    pallas_call x1, Pallas kernels, per_device(): pl.pallas_call(step_kernel, out_shape=(struct(19, 2, 16, 128), struct(3,...  3.4 us
    unnamed x16, local copies, waits for them, and re-layouts  2.34 us
  transfers between devices with their start and end apart: 8, of which 3 were waited for; matrix products, arithmetic and copies ran while one was open for 1% of the time, Pallas kernels for 7%

profile of v1, /device:TPU:6, one launch (start us, length us, event | category | flops | bytes accessed | tf_op | source)
XLA Modules:
  0.0 77.4 jit_solution(2335440997811287067)
XLA Ops:
  0.7 0.1 pad_add_fusion.par
  0.7 0.6 copy-done.1
  1.4 1.0 %copy-done = f32[19,2,16,128]{3,2,1,0:T(8,128)S(1)} copy-done((f32[19,2,16,128]{3,2,1,0:T(8,128)S(1)}, f32[19,2,16,128]{3,2,1,0:T(8,128)}, u32[]{:S(2)}) %copy-start) | copy-done | bytes 311320
  2.3 0.0 copy-start.6
  2.4 0.7 collide.1
  3.1 2.7 %collective-permute-start = (f32[20,16,128]{2,1,0:T(8,128)S(1)}, f32[20,16,128]{2,1,0:T(8,128)S(1)}, u32[]{:S(2)}, u32[]{:S(2)}) collective-permute-start(f32[20,16,128]{2,1,0:T(8,128)S(1)} %get-tuple-element.16), channel_id=1, source_target_pairs={{0,256},{256,0},{512,768},{768,512},{1,257},{257,1},{513,769},{769... | collective-permute-start | bytes 491528 | tf_op jit(solution)/shard_map/ppermute | solution.py:427
  5.8 14.2 %collective-permute-start.1 = (f32[20,16,128]{2,1,0:T(8,128)S(1)}, f32[20,16,128]{2,1,0:T(8,128)S(1)}, u32[]{:S(2)}, u32[]{:S(2)}) collective-permute-start(f32[20,16,128]{2,1,0:T(8,128)S(1)} %get-tuple-element.17), channel_id=1, source_target_pairs={{0,768},{256,512},{512,256},{768,0},{1,769},{257,513},{513,257},{7... | collective-permute-start | bytes 491528 | tf_op jit(solution)/shard_map/ppermute | solution.py:427
  20.0 0.0 copy-done.2
  20.0 0.0 copy-done.3
  20.0 0.0 copy-done.4
  20.0 0.0 copy-done.5
  20.1 4.5 %deposit.1 = f32[4,256,128]{2,1,0:T(8,128)S(1)} custom-call(s32[1,8192]{1,0:T(1,128)S(1)} %bitcast.26, s32[1,8192]{1,0:T(1,128)S(1)} %bitcast.30, s32[1,8192]{1,0:T(1,128)S(1)} %bitcast.28, f32[1,8192]{1,0:T(1,128)S(1)} %bitcast.31, f32[3,8192]{1,0:T(4,128)S(1)} %copy-done.2), custom_call_target="tpu_custom_call" | custom-call | flops 4000000000 | bytes 1000000 | tf_op jit(solution)/shard_map/deposit/pallas_call | solution.py:459
  24.6 0.0 collective-permute-done.xnear
  24.6 0.0 collective-permute-done.1.xfar
  24.6 1.0 %z_pack.1 = (f32[2,16,128]{2,1,0:T(8,128)S(1)}, f32[2,16,128]{2,1,0:T(8,128)S(1)}) custom-call(s32[3]{0:T(128)S(1)} %pad_add_fusion.par, f32[19,2,16,128]{3,2,1,0:T(8,128)S(1)} %get-tuple-element.15.post, f32[2,16,128]{2,1,0:T(8,128)S(1)} %copy-done.1, f32[20,16,128]{2,1,0:T(8,128)S(1)} %collective-permute-done.xnear, ...), custom_call_target="tpu_custom_call" | custom-call | flops 500000 | bytes 1000000 | tf_op jit(solution)/shard_map/z_pack/pallas_call | solution.py:480
  25.6 1.9 %collective-permute-start.2 = (f32[2,16,128]{2,1,0:T(8,128)S(1)}, f32[2,16,128]{2,1,0:T(8,128)S(1)}, u32[]{:S(2)}, u32[]{:S(2)}) collective-permute-start(f32[2,16,128]{2,1,0:T(8,128)S(1)} %get-tuple-element.18), channel_id=1, source_target_pairs={{0,1},{1,0},{2,3},{3,2},{4,5},{5,4},{6,7},{7,6},{8,9},{9,8},{10,11... | collective-permute-start | bytes 49160 | tf_op jit(solution)/shard_map/ppermute | solution.py:427
  27.5 6.4 %collective-permute-start.3 = (f32[2,16,128]{2,1,0:T(8,128)S(1)}, f32[2,16,128]{2,1,0:T(8,128)S(1)}, u32[]{:S(2)}, u32[]{:S(2)}) collective-permute-start(f32[2,16,128]{2,1,0:T(8,128)S(1)} %get-tuple-element.19), channel_id=1, source_target_pairs={{0,15},{1,2},{2,1},{3,4},{4,3},{5,6},{6,5},{7,8},{8,7},{9,10},{10,... | collective-permute-start | bytes 49160 | tf_op jit(solution)/shard_map/ppermute | solution.py:427
  33.9 0.0 collective-permute-done.2.znear
  34.0 5.2 %collective-permute-done.3.zfar = f32[2,16,128]{2,1,0:T(8,128)S(1)} collective-permute-done((f32[2,16,128]{2,1,0:T(8,128)S(1)}, f32[2,16,128]{2,1,0:T(8,128)S(1)}, u32[]{:S(2)}, u32[]{:S(2)}) %collective-permute-start.3) | collective-permute-done | bytes 16416 | tf_op jit(solution)/shard_map/ppermute | solution.py:427
  39.2 0.6 y_pack.1
  39.8 1.9 %collective-permute-start.4 = (f32[264,128]{1,0:T(8,128)S(1)}, f32[264,128]{1,0:T(8,128)S(1)}, u32[]{:S(2)}, u32[]{:S(2)}) collective-permute-start(f32[264,128]{1,0:T(8,128)S(1)} %get-tuple-element.20), channel_id=1, source_target_pairs={{0,16},{16,0},{32,48},{48,32},{64,80},{80,64},{96,112},{112,96},{1... | collective-permute-start | bytes 405512 | tf_op jit(solution)/shard_map/ppermute | solution.py:427
  41.7 13.6 %collective-permute-start.5 = (f32[264,128]{1,0:T(8,128)S(1)}, f32[264,128]{1,0:T(8,128)S(1)}, u32[]{:S(2)}, u32[]{:S(2)}) collective-permute-start(f32[264,128]{1,0:T(8,128)S(1)} %get-tuple-element.21), channel_id=1, source_target_pairs={{0,240},{16,32},{32,16},{48,64},{64,48},{80,96},{96,80},{112,128},... | collective-permute-start | bytes 405512 | tf_op jit(solution)/shard_map/ppermute | solution.py:427
  55.3 0.0 collective-permute-done.4.ynear
  55.3 7.1 %collective-permute-done.5.yfar = f32[264,128]{1,0:T(8,128)S(1)} collective-permute-done((f32[264,128]{1,0:T(8,128)S(1)}, f32[264,128]{1,0:T(8,128)S(1)}, u32[]{:S(2)}, u32[]{:S(2)}) %collective-permute-start.5) | collective-permute-done | bytes 135200 | tf_op jit(solution)/shard_map/ppermute | solution.py:427
  62.4 3.4 %step.1 = (f32[19,2,16,128]{3,2,1,0:T(8,128)}, f32[3,2,16,128]{3,2,1,0:T(8,128)S(1)}, f32[4,2,16,128]{3,2,1,0:T(8,128)S(1)}, f32[4,16,128]{2,1,0:T(8,128)S(1)}, f32[4,16,128]{2,1,0:T(8,128)S(1)}) custom-call(s32[3]{0:T(128)S(1)} %pad_add_fusion.par, f32[19,2,16,128]{3,2,1,0:T(8,128)S(1)} %get-tuple-element.15.post, f32[2,16,128]{2,1,0:T(8,128)S(1)} %copy-done.1, ...), custom_call_target="tpu_custom_call" | custom-call | flops 20000000 | bytes 4000000 | tf_op jit(solution)/shard_map/step/pallas_call | solution.py:502
  65.8 3.3 %collective-permute-start.6 = (f32[4,16,128]{2,1,0:T(8,128)S(1)}, f32[4,16,128]{2,1,0:T(8,128)S(1)}, u32[]{:S(2)}, u32[]{:S(2)}) collective-permute-start(f32[4,16,128]{2,1,0:T(8,128)S(1)} %get-tuple-element.24), channel_id=1, source_target_pairs={{0,256},{256,0},{512,768},{768,512},{1,257},{257,1},{513,769},{769... | collective-permute-start | bytes 98312 | tf_op jit(solution)/shard_map/ppermute | solution.py:427
  69.2 3.2 %collective-permute-start.7 = (f32[4,16,128]{2,1,0:T(8,128)S(1)}, f32[4,16,128]{2,1,0:T(8,128)S(1)}, u32[]{:S(2)}, u32[]{:S(2)}) collective-permute-start(f32[4,16,128]{2,1,0:T(8,128)S(1)} %get-tuple-element.25), channel_id=1, source_target_pairs={{0,768},{256,512},{512,256},{768,0},{1,769},{257,513},{513,257},{7... | collective-permute-start | bytes 98312 | tf_op jit(solution)/shard_map/ppermute | solution.py:427
  72.4 0.9 %drag.1 = f32[3,64,128]{2,1,0:T(8,128)S(1)} custom-call(s32[64,128]{1,0:T(8,128)S(1)} %bitcast.27, s32[64,128]{1,0:T(8,128)S(1)} %bitcast.29, f32[3,64,128]{2,1,0:T(8,128)S(1)} %bitcast.23, f32[3,32,128]{2,1,0:T(8,128)S(1)} %bitcast.25), custom_call_target="tpu_custom_call" | custom-call | flops 5000000 | bytes 1000000 | tf_op jit(solution)/shard_map/drag/pallas_call | solution.py:525
  73.3 0.7 copy.14
  74.0 0.0 collective-permute-done.6.near
  74.0 2.2 %collective-permute-done.7.far = f32[4,16,128]{2,1,0:T(8,128)S(1)} collective-permute-done((f32[4,16,128]{2,1,0:T(8,128)S(1)}, f32[4,16,128]{2,1,0:T(8,128)S(1)}, u32[]{:S(2)}, u32[]{:S(2)}) %collective-permute-start.7) | collective-permute-done | bytes 32800 | tf_op jit(solution)/shard_map/ppermute | solution.py:427
  76.2 1.2 %join.1 = f32[4,2,16,128]{3,2,1,0:T(8,128)} custom-call(s32[3]{0:T(128)S(1)} %pad_add_fusion.par, f32[4,2,16,128]{3,2,1,0:T(8,128)S(1)} %get-tuple-element.23.partial, f32[4,16,128]{2,1,0:T(8,128)S(1)} %collective-permute-done.6.near, f32[4,16,128]{2,1,0:T(8,128)S(1)} %collective-permute-done.7.far), custom_call_target="tpu_custom_call" | custom-call | flops 100000 | bytes 300000 | tf_op jit(solution)/shard_map/join/pallas_call | solution.py:541
  (8 shorter events, 0.0 us)
Async XLA Ops:
  0.6 0.7 copy-start.1
  1.4 1.0 %copy-start = (f32[19,2,16,128]{3,2,1,0:T(8,128)S(1)}, f32[19,2,16,128]{3,2,1,0:T(8,128)}, u32[]{:S(2)}) copy-start(f32[19,2,16,128]{3,2,1,0:T(8,128)} %pops.1) | copy-start | bytes 933892
  2.3 17.7 %copy-start.2 = (f32[3,8192]{1,0:T(4,128)S(1)}, f32[3,8192]{1,0:T(4,128)}, u32[]{:S(2)}) copy-start(f32[3,8192]{1,0:T(4,128)} %velocity.1) | copy-start | bytes 294916
  2.3 17.7 %copy-start.3 = (s32[8192]{0:T(1024)S(1)}, s32[8192]{0:T(1024)}, u32[]{:S(2)}) copy-start(s32[8192]{0:T(1024)} %param.9) | copy-start | bytes 98308
  2.3 17.7 %copy-start.4 = (s32[8192]{0:T(1024)S(1)}, s32[8192]{0:T(1024)}, u32[]{:S(2)}) copy-start(s32[8192]{0:T(1024)} %param.11) | copy-start | bytes 98308
  2.3 17.7 %copy-start.5 = (s32[8192]{0:T(1024)S(1)}, s32[8192]{0:T(1024)}, u32[]{:S(2)}) copy-start(s32[8192]{0:T(1024)} %param.10) | copy-start | bytes 98308
  2.3 17.7 %copy-start.6 = (f32[8192]{0:T(1024)S(1)}, f32[8192]{0:T(1024)}, u32[]{:S(2)}) copy-start(f32[8192]{0:T(1024)} %param.13) | copy-start | bytes 98308
  3.1 21.5 %collective-permute-start = (f32[20,16,128]{2,1,0:T(8,128)S(1)}, f32[20,16,128]{2,1,0:T(8,128)S(1)}, u32[]{:S(2)}, u32[]{:S(2)}) collective-permute-start(f32[20,16,128]{2,1,0:T(8,128)S(1)} %get-tuple-element.16), channel_id=1, source_target_pairs={{0,256},{256,0},{512,768},{768,512},{1,257},{257,1},{513,769},{769... | collective-permute-start | bytes 491528 | tf_op jit(solution)/shard_map/ppermute | solution.py:427
  5.8 18.8 %collective-permute-start.1 = (f32[20,16,128]{2,1,0:T(8,128)S(1)}, f32[20,16,128]{2,1,0:T(8,128)S(1)}, u32[]{:S(2)}, u32[]{:S(2)}) collective-permute-start(f32[20,16,128]{2,1,0:T(8,128)S(1)} %get-tuple-element.17), channel_id=1, source_target_pairs={{0,768},{256,512},{512,256},{768,0},{1,769},{257,513},{513,257},{7... | collective-permute-start | bytes 491528 | tf_op jit(solution)/shard_map/ppermute | solution.py:427
  25.6 8.3 %collective-permute-start.2 = (f32[2,16,128]{2,1,0:T(8,128)S(1)}, f32[2,16,128]{2,1,0:T(8,128)S(1)}, u32[]{:S(2)}, u32[]{:S(2)}) collective-permute-start(f32[2,16,128]{2,1,0:T(8,128)S(1)} %get-tuple-element.18), channel_id=1, source_target_pairs={{0,1},{1,0},{2,3},{3,2},{4,5},{5,4},{6,7},{7,6},{8,9},{9,8},{10,11... | collective-permute-start | bytes 49160 | tf_op jit(solution)/shard_map/ppermute | solution.py:427
  27.5 11.7 %collective-permute-start.3 = (f32[2,16,128]{2,1,0:T(8,128)S(1)}, f32[2,16,128]{2,1,0:T(8,128)S(1)}, u32[]{:S(2)}, u32[]{:S(2)}) collective-permute-start(f32[2,16,128]{2,1,0:T(8,128)S(1)} %get-tuple-element.19), channel_id=1, source_target_pairs={{0,15},{1,2},{2,1},{3,4},{4,3},{5,6},{6,5},{7,8},{8,7},{9,10},{10,... | collective-permute-start | bytes 49160 | tf_op jit(solution)/shard_map/ppermute | solution.py:427
  39.8 15.5 %collective-permute-start.4 = (f32[264,128]{1,0:T(8,128)S(1)}, f32[264,128]{1,0:T(8,128)S(1)}, u32[]{:S(2)}, u32[]{:S(2)}) collective-permute-start(f32[264,128]{1,0:T(8,128)S(1)} %get-tuple-element.20), channel_id=1, source_target_pairs={{0,16},{16,0},{32,48},{48,32},{64,80},{80,64},{96,112},{112,96},{1... | collective-permute-start | bytes 405512 | tf_op jit(solution)/shard_map/ppermute | solution.py:427
  41.7 20.7 %collective-permute-start.5 = (f32[264,128]{1,0:T(8,128)S(1)}, f32[264,128]{1,0:T(8,128)S(1)}, u32[]{:S(2)}, u32[]{:S(2)}) collective-permute-start(f32[264,128]{1,0:T(8,128)S(1)} %get-tuple-element.21), channel_id=1, source_target_pairs={{0,240},{16,32},{32,16},{48,64},{64,48},{80,96},{96,80},{112,128},... | collective-permute-start | bytes 405512 | tf_op jit(solution)/shard_map/ppermute | solution.py:427
  65.8 8.2 %collective-permute-start.6 = (f32[4,16,128]{2,1,0:T(8,128)S(1)}, f32[4,16,128]{2,1,0:T(8,128)S(1)}, u32[]{:S(2)}, u32[]{:S(2)}) collective-permute-start(f32[4,16,128]{2,1,0:T(8,128)S(1)} %get-tuple-element.24), channel_id=1, source_target_pairs={{0,256},{256,0},{512,768},{768,512},{1,257},{257,1},{513,769},{769... | collective-permute-start | bytes 98312 | tf_op jit(solution)/shard_map/ppermute | solution.py:427
  69.2 7.0 %collective-permute-start.7 = (f32[4,16,128]{2,1,0:T(8,128)S(1)}, f32[4,16,128]{2,1,0:T(8,128)S(1)}, u32[]{:S(2)}, u32[]{:S(2)}) collective-permute-start(f32[4,16,128]{2,1,0:T(8,128)S(1)} %get-tuple-element.25), channel_id=1, source_target_pairs={{0,768},{256,512},{512,256},{768,0},{1,769},{257,513},{513,257},{7... | collective-permute-start | bytes 98312 | tf_op jit(solution)/shard_map/ppermute | solution.py:427
